TPU v7x, 256 devices: a whole 4x4x8 slice. The times are simulated.
256 devices in a mesh: row: 16 (over z, core), col: 16 (over y, x).
Axes of the slice: x: 4, y: 4, z: 8, core: 2. Of those that a mesh axis runs over, the one named last changes fastest.
Arguments:
- correlation: float32 [2, 8192, 8192], P(None, 'row', 'col'), may hold values from -16 to 32, as said below
- fock: float32 [2, 8192, 8192], P(None, 'row', 'col'), may hold values from -6 to 6, as said below
Outputs:
- reduced_correlation: float32 [2, 8192, 8192], P(None, 'row', 'col')
- transformed_fock: float32 [2, 8192, 8192], P(None, 'row', 'col')
- panel_factor: float32 [2, 8192, 96], P(None, 'row')
Inputs may be any that keep to these rules, and one draw needn't show every extreme that they name: `correlation`: hermitian and positive definite: part 0 is symmetric, part 1 antisymmetric. `fock`: Hermitian: part 0 is symmetric, part 1 antisymmetric.
All inputs are finite; a program needn't handle non-finite values.
Results may differ from a plain program's by a relative error of at most 0.00013.
Values sent between devices are 32-bit elements; how exact they have to be, the bound alone decides.
A program may use at most 128 MiB of HBM per device.

v0:
```python
import jax
import jax.numpy as jnp
from jax import lax
from jax.sharding import PartitionSpec as P

PANEL = 96


highest = lax.Precision.HIGHEST


def broadcast(shard, axis, root):
    mine = lax.axis_index(axis) == root
    return lax.psum(jnp.where(mine, shard, jnp.zeros_like(shard)), axis)


def sent_together(arrays, axis, dim, along):
    both = jnp.concatenate(arrays, axis=along)
    whole, at, outs = (lax.all_gather(both, axis, axis=dim, tiled=True), 0, [])
    for a in arrays:
        outs.append(lax.slice_in_dim(whole, at, at + a.shape[along], axis=along))
        at += a.shape[along]
    return tuple(outs)


def complex_product(left_real, left_imag, right_real, right_imag):
    real_part = jnp.dot(left_real, right_real, precision=highest) - jnp.dot(
        left_imag, right_imag, precision=highest
    )
    imag_part = jnp.dot(left_real, right_imag, precision=highest) + jnp.dot(
        left_imag, right_real, precision=highest
    )
    return (real_part, imag_part)


def embed_real(real_part, imag_part):
    count = real_part.shape[0]
    upper = jnp.stack([real_part, -imag_part], axis=-1)
    lower = jnp.stack([imag_part, real_part], axis=-1)
    return jnp.stack([upper, lower], axis=1).reshape(2 * count, 2 * count)


def triangular_inverse(real_part, imag_part):
    embedded = embed_real(real_part, imag_part)
    identity = jnp.eye(embedded.shape[0], dtype=embedded.dtype)
    inverse = jax.scipy.linalg.solve_triangular(embedded, identity, lower=True)
    return (inverse[0::2, 0::2], inverse[1::2, 0::2])


def cholesky_inverse(real_part, imag_part):
    factor = jnp.linalg.cholesky(embed_real(real_part, imag_part))
    return triangular_inverse(factor[0::2, 0::2], factor[1::2, 0::2])


def unit_block(count, start):
    return (jnp.arange(count)[:, None] + start == jnp.arange(PANEL)[None, :]).astype(jnp.float32)


def shards(correlation, fock):
    over_real, over_imag = (correlation[0], correlation[1])
    row_count, col_count = over_real.shape
    row_start = lax.axis_index("row") * row_count
    col_start = lax.axis_index("col") * col_count
    panel_spans = (0, PANEL)
    row_parts, col_parts, head_parts, inverse_parts = ([], [], [], [])
    panel_offset, panel_width = panel_spans
    panel_end = panel_offset + panel_width
    left_real = broadcast(over_real[:, panel_offset:panel_end], "col", 0)
    left_imag = broadcast(over_imag[:, panel_offset:panel_end], "col", 0)
    whole_real, whole_imag = sent_together((left_real, left_imag), "row", 0, 1)
    inverse_real, inverse_imag = cholesky_inverse(
        whole_real[panel_offset:panel_end], whole_imag[panel_offset:panel_end]
    )
    every_real, every_imag = complex_product(
        whole_real, whole_imag, inverse_real.T, -inverse_imag.T
    )
    rowf_real = lax.dynamic_slice_in_dim(every_real, row_start, row_count, 0)
    rowf_imag = lax.dynamic_slice_in_dim(every_imag, row_start, row_count, 0)
    colf_real = lax.dynamic_slice_in_dim(every_real, col_start, col_count, 0)
    colf_imag = lax.dynamic_slice_in_dim(every_imag, col_start, col_count, 0)
    headf_real = every_real[:PANEL]
    headf_imag = every_imag[:PANEL]
    update_real, update_imag = complex_product(rowf_real, rowf_imag, colf_real.T, -colf_imag.T)
    over_real = over_real - update_real
    over_imag = over_imag - update_imag
    row_parts.append((rowf_real, rowf_imag))
    col_parts.append((colf_real, colf_imag))
    head_parts.append((headf_real, headf_imag))
    inverse_parts.append((inverse_real, inverse_imag))
    rowall_real = jnp.concatenate([item[0] for item in row_parts], axis=1)
    rowall_imag = jnp.concatenate([item[1] for item in row_parts], axis=1)
    colall_real = jnp.concatenate([item[0] for item in col_parts], axis=1)
    colall_imag = jnp.concatenate([item[1] for item in col_parts], axis=1)
    inverse_real, inverse_imag = inverse_parts[0]
    qrow_real, qrow_imag = complex_product(
        unit_block(row_count, row_start) - rowall_real, -rowall_imag, inverse_real, inverse_imag
    )
    qcol_real, qcol_imag = complex_product(
        unit_block(col_count, col_start) - colall_real, -colall_imag, inverse_real, inverse_imag
    )
    fock_real, fock_imag = (fock[0], fock[1])
    fleft_real, fleft_imag = (
        broadcast(fock_real[:, :PANEL], "col", 0),
        broadcast(fock_imag[:, :PANEL], "col", 0),
    )
    fwhole_real, fwhole_imag = sent_together((fleft_real, fleft_imag), "row", 0, 1)
    fhead_real, fhead_imag = (fwhole_real[:PANEL], fwhole_imag[:PANEL])
    ftop_real = lax.dynamic_slice_in_dim(fwhole_real, col_start, col_count, 0).T
    ftop_imag = -lax.dynamic_slice_in_dim(fwhole_imag, col_start, col_count, 0).T
    step_real, step_imag = complex_product(qrow_real, qrow_imag, ftop_real, ftop_imag)
    partly_real = fock_real + step_real
    partly_imag = fock_imag + step_imag
    edge_real, edge_imag = complex_product(qrow_real, qrow_imag, fhead_real, fhead_imag)
    zleft_real = fleft_real + edge_real
    zleft_imag = fleft_imag + edge_imag
    back_real, back_imag = complex_product(zleft_real, zleft_imag, qcol_real.T, -qcol_imag.T)
    transformed = jnp.stack([partly_real + back_real, partly_imag + back_imag])
    return (jnp.stack([over_real, over_imag]), transformed, jnp.stack([rowall_real, rowall_imag]))


def solution(mesh):
    in_specs = (P(None, "row", "col"), P(None, "row", "col"))
    out_specs = (P(None, "row", "col"), P(None, "row", "col"), P(None, "row", None))
    return jax.shard_map(shards, mesh=mesh, in_specs=in_specs, out_specs=out_specs, check_vma=False)
```

profile of v0, /device:TPU:1, one launch (start us, length us, event | category | flops | bytes accessed | tf_op | source)
XLA Modules:
  0.0 328.9 jit_solution(4215038668590573967)
XLA Ops:
  7.2 3.2 slice_bitcast_fusion.1
  10.4 1.1 slice_bitcast_fusion.3
  11.6 1.9 slice_select_fusion
  13.4 1.8 slice_select_fusion.2
  15.3 100.1 %all-reduce.6.cloned.1.call-done = (f32[512,96]{1,0:T(8,128)}, f32[512,96]{1,0:T(8,128)}, f32[512,96]{1,0:T(8,128)}, f32[512,96]{1,0:T(8,128)}) async-done(((f32[512,96]{1,0:T(8,128)}, f32[512,96]{1,0:T(8,128)}, f32[512,96]{1,0:T(8,128)}, f32[512,96]{1,0:T(8,128)}), (f32[512,96]{1,0:T(8,128)}, f32[512,96]{1,0:T(8,128)}, f32[512,96]{1,0:T(8,128)}, f32[512,96]{1,0:T(8,128)})) %all-reduce.6.cloned.1.call-update) | async-done | bytes 786448 | tf_op jit(solution)/shard_map/psum | solution.py:14
  115.4 2.0 pad_maximum_fusion.2
  117.5 2.0 pad_maximum_fusion.3
  119.6 55.4 %all-gather.3.cloned.1.call-done = f32[8192,192]{1,0:T(8,128)} async-done(((f32[512,192]{1,0:T(8,128)}), f32[8192,192]{1,0:T(8,128)}) %all-gather.3.cloned.1.call-update) | async-done | bytes 6291472 | tf_op jit(solution)/shard_map/all_gather | solution.py:19
  175.0 1.0 negate_bitcast_fusion.1
  176.1 5.1 %copy.12 = f32[96,2,96,2]{3,2,1,0:T(8,128)} copy(f32[96,2,96,2]{2,0,3,1:T(8,128)S(1)} %pad_maximum_fusion.5) | data formatting | bytes 294912 | tf_op jit(solution)/shard_map/stack | solution.py:40
  181.2 8.4 %reshape.45 = f32[192,192]{1,0:T(8,128)S(1)} reshape(f32[96,2,96,2]{3,2,1,0:T(8,128)} %copy.12) | data formatting | bytes 294912 | tf_op jit(solution)/shard_map/reshape | solution.py:40
  189.7 11.7 %cholesky.51 = f32[128,128]{1,0:T(8,128)S(1)} custom-call(f32[128,128]{1,0:T(8,128)S(1)} %cholesky.124), custom_call_target="Cholesky" | custom-call | tf_op jit(solution)/shard_map/jit(cholesky)/cholesky | solution.py:51
  201.5 9.8 %custom-call.15 = f32[1,128,128]{1,2,0:T(8,128)S(1)} custom-call(f32[1,128,128]{2,1,0:T(8,128)S(1)} %get-tuple-element.37), custom_call_target="InvertDiagBlocksLowerTriangular" | custom-call | tf_op jit(solution)/shard_map/jit(cholesky)/cholesky | solution.py:51
  211.7 5.8 %cholesky.110 = f32[64,64]{1,0:T(8,128)S(1)} custom-call(f32[64,64]{1,0:T(8,128)S(1)} %convolution_subtract_fusion.8), custom_call_target="Cholesky" | custom-call | tf_op jit(solution)/shard_map/jit(cholesky)/cholesky | solution.py:51
  220.2 1.3 slice.123
  221.4 1.3 slice.122
  222.8 5.2 %copy.14 = f32[96,2,96,2]{3,2,1,0:T(8,128)} copy(f32[96,2,96,2]{2,0,3,1:T(8,128)S(1)} %pad_maximum_fusion.6) | data formatting | bytes 294912 | tf_op jit(solution)/shard_map/stack | solution.py:40
  228.0 7.9 %reshape.46 = f32[192,192]{1,0:T(8,128)S(1)} reshape(f32[96,2,96,2]{3,2,1,0:T(8,128)} %copy.14) | data formatting | bytes 294912 | tf_op jit(solution)/shard_map/reshape | solution.py:40
  236.1 19.7 %custom-call.16 = f32[2,128,128]{1,2,0:T(8,128)S(1)} custom-call(f32[2,128,128]{2,1,0:T(8,128)S(1)} %pad_maximum_fusion.8), custom_call_target="InvertDiagBlocksLowerTriangular" | custom-call | tf_op jit(solution)/shard_map/jit(_solve_triangular)/triangular_solve | solution.py:46
  256.7 1.3 slice.126
  258.0 1.3 slice.124
  259.3 6.4 %fusion.2 = f32[8192,96]{0,1:T(8,128)S(1)} fusion(f32[8192,192]{1,0:T(8,128)} %all-gather.3.cloned.1.call-done, f32[96,96]{0,1:T(8,128)S(1)} %slice.126), kind=kOutput, calls=%fused_computation.4 | convolution fusion | flops 905978880 | bytes 7376896 | tf_op jit(solution)/shard_map/dot_general | solution.py:30
  265.8 7.9 %convolution_add_fusion = f32[8192,96]{0,1:T(8,128)S(1)} fusion(f32[8192,96]{0,1:T(8,128)S(1)} %fusion.2, f32[96,96]{0,1:T(8,128)S(1)} %slice.124, f32[8192,192]{1,0:T(8,128)} %all-gather.3.cloned.1.call-done), kind=kOutput, calls=%fused_computation | convolution fusion | flops 906756096 | bytes 10522624 | tf_op jit(solution)/shard_map/dot_general | solution.py:30
  274.5 4.5 %fusion.4 = f32[8192,96]{0,1:T(8,128)S(1)} fusion(f32[96,96]{0,1:T(8,128)S(1)} %slice.124, f32[8192,192]{1,0:T(8,128)S(1)} %bitcast.102), kind=kOutput, calls=%fused_computation.6 | convolution fusion | flops 905969664 | bytes 7389184 | tf_op jit(solution)/shard_map/dot_general | solution.py:27
  279.0 4.9 %convolution_subtract_fusion = f32[8192,96]{0,1:T(8,128)S(1)} fusion(f32[8192,96]{0,1:T(8,128)S(1)} %fusion.4, f32[8192,192]{1,0:T(8,128)S(1)} %bitcast.102, f32[96,96]{0,1:T(8,128)S(1)} %slice.126), kind=kOutput, calls=%fused_computation.1 | convolution fusion | flops 906765312 | bytes 10534912 | tf_op jit(solution)/shard_map/dot_general | solution.py:27
  284.7 2.0 fusion.34
  286.7 1.0 fusion.42
  289.2 1.0 convolution_subtract_fusion.5
  290.6 1.1 convolution_add_fusion.6
  291.8 1.8 fusion.18
  293.6 6.3 %fusion.81 = (f32[8192,96]{1,0:T(8,128)S(1)}, f32[8192,96]{1,0:T(8,128)S(1)}) fusion(f32[8192,192]{1,0:T(8,128)} %all-gather.5.cloned.1.call-done), kind=kLoop, calls=%fused_computation.153 | loop fusion | bytes 12582912 | tf_op jit(solution)/shard_map/slice | solution.py:21
  299.9 1.0 fusion.20
  301.0 1.0 fusion.22
  302.0 1.1 fusion.11
  303.1 1.4 fusion.58
  304.5 1.5 fusion.17
  306.0 1.0 fusion.82
  307.0 1.0 fusion.83
  308.0 1.1 fusion.8
  309.1 2.1 fusion.15
  311.3 2.2 fusion.13
  313.4 0.8 pad_maximum_fusion.4
  314.2 1.5 fusion.54
  315.8 1.4 fusion.16
  317.2 1.0 fusion.10
  318.2 1.0 fusion.7
  319.2 1.5 pad_maximum_fusion.1
  320.7 1.5 pad_maximum_fusion
  (73 shorter events, 6.6 us)
Async XLA Ops:
  7.2 3.3 copy-start.1
  7.2 108.2 %all-reduce.6.cloned.1.call-start = ((), (), s32[]{:S(2)}) async-start(), calls=%async_computation.2 | async-start | bytes 2097152 | tf_op jit(solution)/shard_map/psum | solution.py:14
  15.2 159.8 %all-gather.3.cloned.1.call-start = ((), (), s32[]{:S(2)}) async-start(), calls=%async_computation | async-start | bytes 8912896 | tf_op jit(solution)/shard_map/all_gather | solution.py:19
  117.4 176.2 %all-gather.5.cloned.1.call-start = ((), (), s32[]{:S(2)}) async-start(), calls=%async_computation.1 | async-start | bytes 8912896 | tf_op jit(solution)/shard_map/all_gather | solution.py:19
  259.3 29.2 %copy-start.5 = (f32[96,96]{0,1:T(8,128)}, f32[96,96]{0,1:T(8,128)S(1)}, u32[]{:S(2)}) copy-start(f32[96,96]{0,1:T(8,128)S(1)} %slice.124) | copy-start | bytes 110596
  259.3 15.2 %slice-start = ((s8[8388608]{0:T(1024)(128)(4,1)}), s8[4194304]{0:T(1024)(128)(4,1)S(1)}, s32[]{:S(2)}) async-start(s8[8388608]{0:T(1024)(128)(4,1)} %bitcast.101), calls=%async_computation.3 | async-start | bytes 8388608
  265.8 8.7 %slice-start.1 = ((s8[8388608]{0:T(1024)(128)(4,1)}), s8[4194304]{0:T(1024)(128)(4,1)S(1)}, s32[]{:S(2)}) async-start(s8[8388608]{0:T(1024)(128)(4,1)} %bitcast.101), calls=%async_computation.4 | async-start | bytes 8388608
  273.7 18.1 %copy-start.2 = (f32[8192,96]{0,1:T(8,128)}, f32[8192,96]{0,1:T(8,128)S(1)}, u32[]{:S(2)}) copy-start(f32[8192,96]{0,1:T(8,128)S(1)} %convolution_add_fusion) | copy-start | bytes 9437188
  284.0 6.7 %copy-start.3 = (f32[8192,96]{0,1:T(8,128)}, f32[8192,96]{0,1:T(8,128)S(1)}, u32[]{:S(2)}) copy-start(f32[8192,96]{0,1:T(8,128)S(1)} %convolution_subtract_fusion) | copy-start | bytes 9437188
  299.9 2.1 copy-start
  300.9 3.6 %copy-start.9 = (f32[512,96]{1,0:T(8,128)S(1)}, f32[512,96]{1,0:T(8,128)}, u32[]{:S(2)}) copy-start(f32[512,96]{1,0:T(8,128)} %get-tuple-element.26) | copy-start | bytes 589828
  300.9 5.1 %copy-start.6 = (f32[512,96]{0,1:T(8,128)S(1)}, f32[512,96]{0,1:T(8,128)}, u32[]{:S(2)}) copy-start(f32[512,96]{0,1:T(8,128)} %convolution_subtract_fusion.5) | copy-start | bytes 589828
  302.0 5.0 %copy-start.7 = (f32[96,512]{1,0:T(8,128)S(1)}, f32[96,512]{1,0:T(8,128)}, u32[]{:S(2)}) copy-start(f32[96,512]{1,0:T(8,128)} %fusion.18) | copy-start | bytes 589828
  306.0 3.1 copy-start.4
  309.1 4.3 %copy-start.10 = (f32[1,512,96]{1,2,0:T(8,128)S(1)}, f32[1,512,96]{1,2,0:T(8,128)}, u32[]{:S(2)}) copy-start(f32[1,512,96]{1,2,0:T(8,128)} %dynamic-slice_bitcast_fusion) | copy-start | bytes 589828
  309.1 4.3 %copy-start.11 = (f32[1,512,96]{1,2,0:T(8,128)S(1)}, f32[1,512,96]{1,2,0:T(8,128)}, u32[]{:S(2)}) copy-start(f32[1,512,96]{1,2,0:T(8,128)} %dynamic-slice_bitcast_fusion.1) | copy-start | bytes 589828
  311.3 4.5 %copy-start.8 = (f32[512,96]{1,0:T(8,128)S(1)}, f32[512,96]{1,0:T(8,128)}, u32[]{:S(2)}) copy-start(f32[512,96]{1,0:T(8,128)} %get-tuple-element.25) | copy-start | bytes 589828
Sparse Core Ops, SparseCore 0:
  15.4 99.9 all-reduce.5
  117.8 57.2 all-gather.2
  177.4 54.3 all-gather.4
where the time goes:
time: 332 us; the launch traced here: 329 us
  waiting for transfers between devices  156 us (47%)
  other arithmetic  61.2 us (18%)
  matrix products  52.1 us (16%)
  local copies, waits for them, and re-layouts  44.1 us (13%)
  between operations  15.9 us (5%)
    psum x1, waiting for transfers between devices, broadcast(): return lax.psum(jnp.where(mine, shard, jnp.zeros_like(shard)), axis)  100 us
    all_gather x2, waiting for transfers between devices, sent_together(): whole, at, outs = (lax.all_gather(both, axis, axis=dim, tiled=True), 0, [])  55.4 us
    another operation x7, other arithmetic, cholesky_inverse(): factor = jnp.linalg.cholesky(embed_real(real_part, imag_part))  28.7 us
    another operation x7, other arithmetic, triangular_inverse(): inverse = jax.scipy.linalg.solve_triangular(embedded, identity, lower=True)  19.8 us
    dot_general x7, matrix products, complex_product(): jnp.dot(left_imag, right_real, precision=highest)  16.5 us
    reshape x3, local copies, waits for them, and re-layouts, embed_real(): return jnp.stack([upper, lower], axis=1).reshape(2 * count, 2 * count)  16.4 us
    dot_general x7, matrix products, complex_product(): jnp.dot(left_imag, right_imag, precision=highest)  12 us
    dot_general x7, matrix products, complex_product(): jnp.dot(left_real, right_imag, precision=highest)  11.7 us
  transfers between devices with their start and end apart: 3, of which 2 were waited for; matrix products, arithmetic and copies ran while one was open for 36% of the time, Pallas kernels for 0%

commit v1 on v0

v1 whole, which is shorter than its diff:
```python
import jax
import jax.numpy as jnp
from jax import lax
from jax.experimental import pallas as pl
from jax.experimental.pallas import tpu as pltpu
from jax.sharding import PartitionSpec as P

PANEL = 96
LANES = 128
MESH = pl.DeviceIdType.MESH

INTO = (-1, 0, 0, 0, 2, 1, 0, 0, 2, 1, 1, 0, 2, 3, 3, 0)
DEPTH = (0, 1, 2, 3, 3, 2, 3, 4, 4, 3, 4, 5, 3, 2, 3, 4)
STEP = ((1, 0), (0, 1), (-1, 0), (0, -1))

TREE_CHUNKS = 8
TREE_ROWS = 32
CHAIN_CHUNKS = 12
CHAIN_ROWS = 16
TREE_LAG = 3
CHAIN_LAG = 3
SLOTS = 25


def rotated(x, y, turns):
    for _ in range(turns % 4):
        x, y = -y % 4, x % 4
    return x, y


def tree_tables():
    depth = [[0] * 16 for _ in range(4)]
    send = [[-1] * 16 for _ in range(4)]
    for tree in range(4):
        for chip in range(16):
            x, y = rotated(chip % 4, chip // 4, -tree)
            depth[tree][chip] = DEPTH[y * 4 + x]
            if chip:
                way = (INTO[y * 4 + x] + tree) % 4
                px, py = (chip % 4 - STEP[way][0]) % 4, (chip // 4 - STEP[way][1]) % 4
                assert send[way][py * 4 + px] == -1
                send[way][py * 4 + px] = tree
    return depth, send


def lookup(index, table):
    value = jnp.int32(0)
    for k, entry in enumerate(table):
        if entry:
            value = value + jnp.where(index == k, jnp.int32(entry), jnp.int32(0))
    return value


def spread(corr, fock, rowp, colp, small, wr, wi, dv, local_sem, tree_send, tree_recv, chain_send, chain_recv, small_send, small_recv):
    r, c = lax.axis_index("row"), lax.axis_index("col")
    z, core = r // 2, r % 2
    y, x = c // 4, c % 4
    root = (r == 0) & (c == 0)
    depth_table, send_table = tree_tables()

    def along_x(step):
        return (r, 4 * y + (x + step) % 4)

    def along_y(step):
        return (r, 4 * ((y + step) % 4) + x)

    def along_z(step):
        return (2 * ((z + step) % 8) + core, c)

    partner = (r + 1 - 2 * core, c)

    barrier = pltpu.get_barrier_semaphore()
    greeted = [along_x(s) for s in (1, 2, 3)] + [along_y(s) for s in (1, 2, 3)] + [along_z(s) for s in range(1, 8)] + [partner]
    for peer in greeted:
        pl.semaphore_signal(barrier, inc=1, device_id=peer, device_id_type=MESH)

    row_copies = [pltpu.make_async_copy(src.at[:, :, pl.ds(0, LANES)], rowp.at[i], local_sem.at[i]) for i, src in enumerate((corr, fock))]
    col_copies = [pltpu.make_async_copy(src.at[:, pl.ds(0, PANEL), :], colp.at[i], local_sem.at[2 + i]) for i, src in enumerate((corr, fock))]

    @pl.when(c == 0)
    def _():
        for copy in row_copies:
            copy.start()

    @pl.when(r == 0)
    def _():
        for copy in col_copies:
            copy.start()

    @pl.when(c == 0)
    def _():
        for copy in row_copies:
            copy.wait()

    @pl.when(r == 0)
    def _():
        for copy in col_copies:
            copy.wait()

    neighbours = (along_x(1), along_y(1), along_x(3), along_y(3))

    def tree_copy(tree, chunk, way):
        rows = pl.ds(pl.multiple_of(LANES * tree + TREE_ROWS * (chunk % 4), TREE_ROWS), TREE_ROWS)
        part = rowp.at[chunk // 4, :, rows, :]
        return pltpu.make_async_remote_copy(
            src_ref=part, dst_ref=part, send_sem=tree_send.at[way, chunk], recv_sem=tree_recv.at[tree, chunk],
            device_id=neighbours[way], device_id_type=MESH)

    chain_peers = (along_z(1), along_z(7), partner)

    def chain_copy(chunk, way):
        rows = pl.ds(pl.multiple_of(CHAIN_ROWS * (chunk % 6), CHAIN_ROWS), CHAIN_ROWS)
        part = colp.at[chunk // 6, :, rows, :]
        return pltpu.make_async_remote_copy(
            src_ref=part, dst_ref=part, send_sem=chain_send.at[way, chunk], recv_sem=chain_recv.at[chunk],
            device_id=chain_peers[way], device_id_type=MESH)

    def small_copy(which, index, peer):
        return pltpu.make_async_remote_copy(
            src_ref=small.at[which], dst_ref=small.at[which], send_sem=small_send.at[which, index],
            recv_sem=small_recv.at[which], device_id=peer, device_id_type=MESH)

    def small_groups(which):
        far_z = [small_copy(which, i, along_z(s)) for i, s in enumerate((4, 3, 5, 2, 6, 1, 7))]
        far_x = [small_copy(which, 7 + i, along_x(s)) for i, s in enumerate((2, 1, 3))]
        far_y = [small_copy(which, 10 + i, along_y(s)) for i, s in enumerate((2, 1, 3))]
        near = [small_copy(which, 13, partner)]
        return (((root, far_z), ((c == 0) & (core == 0), far_x), ((y == 0) & (core == 0), far_y), (core == 0, near)))

    def small_forward(which):
        for condition, copies in small_groups(which):
            @pl.when(condition)
            def _():
                for copy in copies:
                    copy.start()

    def small_event(which):
        small_copy(which, 13, partner).wait_recv()
        small_forward(which)

    send_tree = [lookup(c, [entry + 1 for entry in send_table[way]]) - 1 for way in range(4)]
    chain_up = (core == 0) & (z < 4)
    chain_down = (core == 0) & ((z == 0) | (z > 5))
    chain_ways = (chain_up, chain_down, core == 0)

    @pl.when(root)
    def _():
        lane = lax.broadcasted_iota(jnp.int32, (PANEL, LANES), 1)
        row = lax.broadcasted_iota(jnp.int32, (PANEL, LANES), 0)
        inside = lane < PANEL
        wr[...] = jnp.where(inside, rowp[0, 0, pl.ds(0, PANEL), :], 0.0)
        wi[...] = jnp.zeros_like(wi)
        wi[pl.ds(0, PANEL), :] = jnp.where(inside, rowp[0, 1, pl.ds(0, PANEL), :], 0.0)
        head_real = rowp[1, 0, pl.ds(0, PANEL), :]
        head_imag = rowp[1, 1, pl.ds(0, PANEL), :]
        small[0] = jnp.where(inside, jnp.where(lane <= row, head_real, head_imag), 0.0)

        def eliminate(block, carry):
            for j in range(8):
                k = block * 8 + j
                at = lane == j
                row_real = wr[pl.ds(k, 1), :]
                row_imag = wi[pl.ds(k, 1), :]
                pivot = jnp.broadcast_to(row_real[:, j:j + 1], (1, LANES))
                dv[pl.ds(k, 1), :] = pivot
                scale = 1.0 / pivot
                here = at[0:1, :]
                row_real = jnp.where(here, scale, row_real * scale)
                row_imag = jnp.where(here, 0.0, row_imag * scale)
                real, imag = wr[...], wi[pl.ds(0, PANEL), :]
                below = row > k
                col_real = jnp.where(below, jnp.broadcast_to(real[:, j:j + 1], (PANEL, LANES)), 0.0)
                col_imag = jnp.where(below, jnp.broadcast_to(imag[:, j:j + 1], (PANEL, LANES)), 0.0)
                wr[...] = jnp.where(at, 0.0, real) - (col_real * row_real - col_imag * row_imag)
                wi[pl.ds(0, PANEL), :] = jnp.where(at, 0.0, imag) - (col_real * row_imag + col_imag * row_real)
            wr[...] = pltpu.roll(wr[...], LANES - 8, 1)
            wi[pl.ds(0, PANEL), :] = pltpu.roll(wi[pl.ds(0, PANEL), :], LANES - 8, 1)

            @pl.when(block == 4)
            def _():
                pl.semaphore_wait(barrier, len(greeted))
                small_forward(0)

            @pl.when((block >= 5) & (block < 9))
            def _():
                for i in range(2):
                    for way in range(4):
                        tree_copy(way, 2 * (block - 5) + i, way).start()
                for i in range(3):
                    for way in range(3):
                        chain_copy(3 * (block - 5) + i, way).start()

            return carry

        lax.fori_loop(0, PANEL // 8, eliminate, 0)
        pivots = dv[...]
        scale = lax.rsqrt(pivots)
        scale = scale * (1.5 - 0.5 * pivots * scale * scale)
        eye = jnp.where(lane == row, 1.0, 0.0)
        inverse_real = (pltpu.roll(wr[...], PANEL, 1) + eye) * scale
        wi[pl.ds(0, PANEL), :] = pltpu.roll(wi[pl.ds(0, PANEL), :], PANEL, 1) * scale
        small[1] = inverse_real + wi[...].T[0:PANEL, :]
        small_forward(1)

    @pl.when(jnp.logical_not(root))
    def _():
        pl.semaphore_wait(barrier, len(greeted))
        depth = [lookup(c, depth_table[tree]) for tree in range(4)]
        chain_depth = jnp.where(z <= 4, z, 8 - z)
        small_slot = jnp.where(c == 0, 7, jnp.where(y == 0, 11, 15))

        def slot(s, carry):
            for tree in range(4):
                chunk = s - TREE_LAG * depth[tree]

                @pl.when((chunk >= 0) & (chunk < TREE_CHUNKS))
                def _():
                    @pl.when(c != 0)
                    def _():
                        tree_copy(tree, chunk, 0).wait_recv()

                    for way in range(4):
                        @pl.when(send_tree[way] == tree)
                        def _():
                            tree_copy(tree, chunk, way).start()

            link = s - CHAIN_LAG * chain_depth

            @pl.when((core == 0) & (link >= 0) & (link < CHAIN_CHUNKS))
            def _():
                @pl.when(z != 0)
                def _():
                    chain_copy(link, 0).wait_recv()

                for way in range(3):
                    @pl.when(chain_ways[way])
                    def _():
                        chain_copy(link, way).start()

            @pl.when(s == small_slot)
            def _():
                small_event(0)

            return carry

        lax.fori_loop(0, SLOTS, slot, 0)
        small_event(1)

        @pl.when(core == 1)
        def _():
            def arrived(chunk, carry):
                chain_copy(chunk, 2).wait_recv()
                return carry

            lax.fori_loop(0, CHAIN_CHUNKS, arrived, 0)

    for way in range(4):
        @pl.when(send_tree[way] >= 0)
        def _():
            def sent(chunk, carry):
                tree_copy(0, chunk, way).wait_send()
                return carry

            lax.fori_loop(0, TREE_CHUNKS, sent, 0)

    for way in range(3):
        @pl.when(chain_ways[way])
        def _():
            def sent(chunk, carry):
                chain_copy(chunk, way).wait_send()
                return carry

            lax.fori_loop(0, CHAIN_CHUNKS, sent, 0)

    for which in range(2):
        for condition, copies in small_groups(which):
            @pl.when(condition)
            def _():
                for copy in copies:
                    copy.wait_send()


def halves(value):
    high = value.astype(jnp.bfloat16)
    return high, (value - high.astype(jnp.float32)).astype(jnp.bfloat16)


def product(left, right):
    (left_high, left_low), (right_high, right_low) = left, right

    def dot(a, b):
        return jnp.dot(a, b, preferred_element_type=jnp.float32)

    return dot(left_high, right_high) + (dot(left_low, right_high) + dot(left_high, right_low))


def block_matrix(a, b, c, d):
    return jnp.concatenate([jnp.concatenate([a, b], axis=1), jnp.concatenate([c, d], axis=1)], axis=0)


TILE = 128


def update(corr, fock, rowp, colp, small, over, transformed, panel, cbuf, fbuf, pbuf, over_left, over_right, fock_left, fock_right, in_sem, out_sem, panel_sem):
    r, c = lax.axis_index("row"), lax.axis_index("col")
    loads = [pltpu.make_async_copy(src, dst, in_sem.at[i]) for i, (src, dst) in enumerate(((corr, cbuf), (fock, fbuf)))]
    for load in loads:
        load.start()

    size = rowp.shape[2]
    width = colp.shape[3]
    row = lax.broadcasted_iota(jnp.int32, (LANES, LANES), 0)
    col = lax.broadcasted_iota(jnp.int32, (LANES, LANES), 1)
    rest = jnp.zeros((LANES - PANEL, LANES), jnp.float32)
    packed = jnp.concatenate([small[1], rest], axis=0)
    turned = packed.T
    inv_real = jnp.where(row >= col, packed, 0.0)
    inv_imag = jnp.where(row > col, turned, 0.0)
    inv_real_t = jnp.where(row <= col, turned, 0.0)
    inv_imag_t = jnp.where(row < col, packed, 0.0)
    right_adjoint = halves(block_matrix(inv_real_t, -inv_imag_t, inv_imag_t, inv_real_t))
    right_inverse = halves(block_matrix(inv_real, inv_imag, -inv_imag, inv_real))
    left_inverse = halves(block_matrix(inv_real, -inv_imag, inv_imag, inv_real))
    left_adjoint = halves(block_matrix(inv_real_t, inv_imag_t, -inv_imag_t, inv_real_t))

    gap = jnp.zeros((LANES - PANEL, width), jnp.float32)

    def top(which):
        return jnp.concatenate([colp[which, 0], gap, colp[which, 1], gap], axis=0)

    factor = product(halves(jnp.concatenate([rowp[0, 0], rowp[0, 1]], axis=1)), right_adjoint)
    pbuf[0] = factor[:, 0:PANEL]
    pbuf[1] = factor[:, LANES:LANES + PANEL]
    panel_out = pltpu.make_async_copy(pbuf, panel, panel_sem)
    panel_out.start()
    over_left[0], over_left[1] = halves(factor)
    across = product(left_inverse, halves(top(0)))

    def right_side(value):
        real, imag = value[0:LANES], value[LANES:2 * LANES]
        return block_matrix(real, imag, -imag, real)

    over_right[0], over_right[1] = halves(right_side(across))

    out_copies = []

    def outer_tiles(left, right, buffer, target, which, sign):
        for tile in range(size // TILE):
            rows = pl.ds(tile * TILE, TILE)
            change = product((left[0, rows, :], left[1, rows, :]), (right[0], right[1]))
            for part in range(2):
                piece = change[:, part * width:(part + 1) * width]
                old = buffer[part, rows, :]
                buffer[part, rows, :] = old + piece if sign > 0 else old - piece
            copy = pltpu.make_async_copy(buffer.at[:, rows, :], target.at[:, rows, :], out_sem.at[which, tile])
            copy.start()
            out_copies.append(copy)

    loads[0].wait()
    outer_tiles(over_left, over_right, cbuf, over, 0, -1)

    wide_row = lax.broadcasted_iota(jnp.int32, (size, 2 * LANES), 0) + r * size
    wide_lane = lax.broadcasted_iota(jnp.int32, (size, 2 * LANES), 1)
    unit = jnp.where((wide_row == wide_lane) & (wide_lane < PANEL), 1.0, 0.0)
    trans = product(halves(unit - factor), right_inverse)
    fock_left[0, :, 0:2 * LANES], fock_left[1, :, 0:2 * LANES] = halves(trans)
    fock_left[0, :, 2 * LANES:4 * LANES], fock_left[1, :, 2 * LANES:4 * LANES] = halves(jnp.concatenate([rowp[1, 0], rowp[1, 1]], axis=1))
    tall_row = lax.broadcasted_iota(jnp.int32, (2 * LANES, width), 0)
    tall_lane = lax.broadcasted_iota(jnp.int32, (2 * LANES, width), 1) + c * width
    unit = jnp.where((tall_row == tall_lane) & (tall_row < PANEL), 1.0, 0.0)
    trans_across = product(left_adjoint, halves(unit - across))

    packed = jnp.concatenate([small[0], rest], axis=0)
    turned = packed.T
    head_real = jnp.where(row >= col, packed, turned)
    head_imag = jnp.where(row < col, packed, jnp.where(row > col, -turned, 0.0))
    head = halves(block_matrix(head_real, -head_imag, head_imag, head_real))
    middle = top(1) + product(head, halves(trans_across))
    fock_right[0, 0:2 * LANES, :], fock_right[1, 0:2 * LANES, :] = halves(right_side(middle))
    fock_right[0, 2 * LANES:4 * LANES, :], fock_right[1, 2 * LANES:4 * LANES, :] = halves(right_side(trans_across))

    loads[1].wait()
    outer_tiles(fock_left, fock_right, fbuf, transformed, 1, 1)
    panel_out.wait()
    for copy in out_copies:
        copy.wait()


def shards(correlation, fock):
    rows, cols = correlation.shape[1:]
    f32, bf16 = jnp.float32, jnp.bfloat16
    hbm, vmem = pl.BlockSpec(memory_space=pl.ANY), pl.BlockSpec(memory_space=pltpu.VMEM)
    dma = pltpu.SemaphoreType.DMA
    rowp, colp, small = pl.pallas_call(
        spread,
        name="spread",
        out_shape=(
            jax.ShapeDtypeStruct((2, 2, rows, LANES), f32),
            jax.ShapeDtypeStruct((2, 2, PANEL, cols), f32),
            jax.ShapeDtypeStruct((2, PANEL, LANES), f32),
        ),
        in_specs=[hbm, hbm],
        out_specs=(vmem, vmem, vmem),
        scratch_shapes=[
            pltpu.VMEM((PANEL, LANES), f32),
            pltpu.VMEM((LANES, LANES), f32),
            pltpu.VMEM((PANEL, LANES), f32),
            dma((4,)),
            dma((4, TREE_CHUNKS)),
            dma((4, TREE_CHUNKS)),
            dma((3, CHAIN_CHUNKS)),
            dma((CHAIN_CHUNKS,)),
            dma((2, 14)),
            dma((2,)),
        ],
        compiler_params=pltpu.CompilerParams(collective_id=0, has_side_effects=True),
    )(correlation, fock)
    return pl.pallas_call(
        update,
        name="update",
        out_shape=(
            jax.ShapeDtypeStruct((2, rows, cols), f32),
            jax.ShapeDtypeStruct((2, rows, cols), f32),
            jax.ShapeDtypeStruct((2, rows, PANEL), f32),
        ),
        in_specs=[hbm, hbm, vmem, vmem, vmem],
        out_specs=(hbm, hbm, hbm),
        scratch_shapes=[
            pltpu.VMEM((2, rows, cols), f32),
            pltpu.VMEM((2, rows, cols), f32),
            pltpu.VMEM((2, rows, PANEL), f32),
            pltpu.VMEM((2, rows, 2 * LANES), bf16),
            pltpu.VMEM((2, 2 * LANES, 2 * cols), bf16),
            pltpu.VMEM((2, rows, 4 * LANES), bf16),
            pltpu.VMEM((2, 4 * LANES, 2 * cols), bf16),
            dma((2,)),
            dma((2, rows // TILE)),
            dma,
        ],
        compiler_params=pltpu.CompilerParams(vmem_limit_bytes=48 * 1024 * 1024),
    )(correlation, fock, rowp, colp, small)


def solution(mesh):
    in_specs = (P(None, "row", "col"), P(None, "row", "col"))
    out_specs = (P(None, "row", "col"), P(None, "row", "col"), P(None, "row", None))
    return jax.shard_map(shards, mesh=mesh, in_specs=in_specs, out_specs=out_specs, check_vma=False)
```

time: 332 us -> 50.4 us (0.15)
  the two profiles are of different devices: /device:TPU:1 before, /device:TPU:139 now
where the time goes in v1:
time: 50.4 us; the launch traced here: 50.1 us
  Pallas kernels  45.3 us (90%)
  local copies, waits for them, and re-layouts  4.19 us (8%)
  between operations  0.67 us (1%)
    pallas_call x1, Pallas kernels, shards(): pl.pallas_call(spread, name='spread', out_shape=(jax.ShapeDtypeStruct((2,...  39.3 us
    pallas_call x1, Pallas kernels, shards(): pl.pallas_call(update, name='update', out_shape=(jax.ShapeDtypeStruct((2,...  5.97 us
    unnamed x8, local copies, waits for them, and re-layouts  3.25 us

profile of v1, /device:TPU:139, one launch (start us, length us, event | category | flops | bytes accessed | tf_op | source)
XLA Modules:
  0.0 50.1 jit_solution(4917055030040910381)
XLA Ops:
  0.6 0.0 copy-start
  0.6 39.3 %spread.1 = (f32[2,2,512,128]{3,2,1,0:T(8,128)}, f32[2,2,96,512]{3,2,1,0:T(8,128)}, f32[2,96,128]{2,1,0:T(8,128)}) custom-call(f32[2,512,512]{2,1,0:T(8,128)} %corr.3, f32[2,512,512]{2,1,0:T(8,128)} %fock.3), custom_call_target="tpu_custom_call" | custom-call | tf_op jit(solution)/shard_map/spread/pallas_call | solution.py:394
  40.0 0.0 copy-done
  40.0 0.0 copy-start.1
  40.0 1.2 %copy-done.1 = f32[2,2,512,128]{3,2,1,0:T(8,128)S(1)} copy-done((f32[2,2,512,128]{3,2,1,0:T(8,128)S(1)}, f32[2,2,512,128]{3,2,1,0:T(8,128)}, u32[]{:S(2)}) %copy-start.1) | copy-done | bytes 1048600
  41.2 0.0 copy-start.2
  41.2 1.1 %copy-done.2 = f32[2,2,96,512]{3,2,1,0:T(8,128)S(1)} copy-done((f32[2,2,96,512]{3,2,1,0:T(8,128)S(1)}, f32[2,2,96,512]{3,2,1,0:T(8,128)}, u32[]{:S(2)}) %copy-start.2) | copy-done | bytes 786456
  42.3 0.0 copy-start.3
  42.3 0.9 %copy-done.3 = f32[2,96,128]{2,1,0:T(8,128)S(1)} copy-done((f32[2,96,128]{2,1,0:T(8,128)S(1)}, f32[2,96,128]{2,1,0:T(8,128)}, u32[]{:S(2)}) %copy-start.3) | copy-done | bytes 98328
  43.2 6.0 %update.1 = (f32[2,512,512]{2,1,0:T(8,128)}, f32[2,512,512]{2,1,0:T(8,128)}, f32[2,512,96]{2,1,0:T(8,128)S(1)}) custom-call(f32[2,512,512]{2,1,0:T(8,128)S(1)} %copy-done, f32[2,512,512]{2,1,0:T(8,128)} %fock.3, f32[2,2,512,128]{3,2,1,0:T(8,128)S(1)} %copy-done.1, f32[2,2,96,512]{3,2,1,0:T(8,128)S(1)} %copy-done.2, f32[2,96,128]{2,1,0:T(8,128)S(1)} %copy-done.3), custom_call_target="tpu_custom_call" | custom-call | tf_op jit(solution)/shard_map/update/pallas_call | solution.py:418
  49.2 0.9 %copy.5 = f32[2,512,96]{1,2,0:T(8,128)} copy(f32[2,512,96]{2,1,0:T(8,128)S(1)} %get-tuple-element.11) | data formatting | bytes 786432 | tf_op jit(solution)/shard_map/update/pallas_call | solution.py:418
Async XLA Ops:
  0.6 39.3 %copy-start = (f32[2,512,512]{2,1,0:T(8,128)S(1)}, f32[2,512,512]{2,1,0:T(8,128)}, u32[]{:S(2)}) copy-start(f32[2,512,512]{2,1,0:T(8,128)} %corr.3) | copy-start | bytes 6291460
  40.0 1.2 %copy-start.1 = (f32[2,2,512,128]{3,2,1,0:T(8,128)S(1)}, f32[2,2,512,128]{3,2,1,0:T(8,128)}, u32[]{:S(2)}) copy-start(f32[2,2,512,128]{3,2,1,0:T(8,128)} %get-tuple-element.6.rowp) | copy-start | bytes 3145732
  41.2 1.1 %copy-start.2 = (f32[2,2,96,512]{3,2,1,0:T(8,128)S(1)}, f32[2,2,96,512]{3,2,1,0:T(8,128)}, u32[]{:S(2)}) copy-start(f32[2,2,96,512]{3,2,1,0:T(8,128)} %get-tuple-element.7.colp) | copy-start | bytes 2359300
  42.3 0.9 %copy-start.3 = (f32[2,96,128]{2,1,0:T(8,128)S(1)}, f32[2,96,128]{2,1,0:T(8,128)}, u32[]{:S(2)}) copy-start(f32[2,96,128]{2,1,0:T(8,128)} %get-tuple-element.8.small) | copy-start | bytes 294916

commit v2 on v1

v2 whole, which is shorter than its diff:
```python
import jax
import jax.numpy as jnp
from jax import lax
from jax.experimental import pallas as pl
from jax.experimental.pallas import tpu as pltpu
from jax.sharding import PartitionSpec as P

PANEL = 96
LANES = 128
MESH = pl.DeviceIdType.MESH

INTO = (-1, 0, 0, 0, 2, 1, 0, 0, 2, 1, 1, 0, 2, 3, 3, 0)
DEPTH = (0, 1, 2, 3, 3, 2, 3, 4, 4, 3, 4, 5, 3, 2, 3, 4)
STEP = ((1, 0), (0, 1), (-1, 0), (0, -1))

TREE_ROWS = 32
TREE_CHUNKS = 2 * LANES // TREE_ROWS
CHAIN_ROWS = 16
CHAIN_CHUNKS = 2 * PANEL // CHAIN_ROWS
TREE_LAG = 5
CHAIN_LAG = 5
CHAIN_START = 3
DOWN_START = 4
STAGE_SLOTS = 5
SMALL_SLOT = 9
SLOTS = max(5 * TREE_LAG + TREE_CHUNKS, 4 * CHAIN_LAG + CHAIN_CHUNKS + CHAIN_START + DOWN_START, 4 * STAGE_SLOTS + SMALL_SLOT + 1)
GREET_AT = 46
HEAD_AT = 78


def rotated(x, y, turns):
    for _ in range(turns % 4):
        x, y = -y % 4, x % 4
    return x, y


def tree_tables():
    depth = [[0] * 16 for _ in range(4)]
    send = [[-1] * 16 for _ in range(4)]
    for tree in range(4):
        for chip in range(16):
            x, y = rotated(chip % 4, chip // 4, -tree)
            depth[tree][chip] = DEPTH[y * 4 + x]
            if chip:
                way = (INTO[y * 4 + x] + tree) % 4
                px, py = (chip % 4 - STEP[way][0]) % 4, (chip // 4 - STEP[way][1]) % 4
                assert send[way][py * 4 + px] == -1
                send[way][py * 4 + px] = tree
    return depth, send


def lookup(index, table):
    value = jnp.int32(0)
    for k, entry in enumerate(table):
        if entry:
            value = value + jnp.where(index == k, jnp.int32(entry), jnp.int32(0))
    return value


def spread(corr, fock, rowp, colp, small, wr, wi, dv, head, local_sem, tree_send, tree_recv, chain_send, chain_recv, small_send, small_recv, chain_ready, chain_ready_down, small_ready):
    r, c = lax.axis_index("row"), lax.axis_index("col")
    z, core = r // 2, r % 2
    y, x = c // 4, c % 4
    root = (r == 0) & (c == 0)
    depth_table, send_table = tree_tables()

    def along_x(step):
        return (r, 4 * y + (x + step) % 4)

    def along_y(step):
        return (r, 4 * ((y + step) % 4) + x)

    def along_z(step):
        return (2 * ((z + step) % 8) + core, c)

    partner = (r + 1 - 2 * core, c)

    barrier = pltpu.get_barrier_semaphore()
    greeted = [along_x(s) for s in (1, 2, 3)] + [along_y(s) for s in (1, 2, 3)] + [partner]
    for peer in greeted:
        pl.semaphore_signal(barrier, inc=1, device_id=peer, device_id_type=MESH)

    on_chain = core == jnp.where(c == 0, 1, 0)
    edge = (c == 0) & (core == 0)
    chain_up, chain_down = on_chain & (z < 4), on_chain & ((z == 0) | (z > 5))
    z_greetings = (
        (chain_up, 1), (chain_down, 7),
        (edge & ((z == 0) | (z == 3)), 1), (edge & (z == 0), 2), (edge & (z == 0), 3),
        (edge & ((z == 0) | (z == 6)), 7), (edge & (z == 0), 6))
    for condition, step in z_greetings:
        @pl.when(condition)
        def _():
            pl.semaphore_signal(barrier, inc=1, device_id=along_z(step), device_id_type=MESH)

    heard = len(greeted) + jnp.where((z > 0) & (on_chain | edge), 1, 0)

    def answer():
        pl.semaphore_wait(barrier, heard)

        @pl.when(on_chain & (z > 0) & (z <= 4))
        def _():
            pl.semaphore_signal(chain_ready, inc=1, device_id=along_z(7), device_id_type=MESH)

        @pl.when(on_chain & (z > 4))
        def _():
            pl.semaphore_signal(chain_ready_down, inc=1, device_id=along_z(1), device_id_type=MESH)

        @pl.when(edge & (z > 0))
        def _():
            back = jnp.where((z == 1) | (z == 4), 7, jnp.where(z == 2, 6, jnp.where(z == 3, 5, jnp.where(z == 6, 2, 1))))
            pl.semaphore_signal(small_ready, inc=1, device_id=along_z(back), device_id_type=MESH)

    head_copies = [pltpu.make_async_copy(corr.at[:, pl.ds(0, PANEL), pl.ds(0, LANES)], head, local_sem.at[4])]
    row_copies = [pltpu.make_async_copy(src.at[:, :, pl.ds(0, LANES)], rowp.at[i], local_sem.at[i]) for i, src in enumerate((corr, fock))]
    col_copies = [pltpu.make_async_copy(src.at[:, pl.ds(0, PANEL), :], colp.at[i], local_sem.at[2 + i]) for i, src in enumerate((corr, fock))]

    @pl.when(root)
    def _():
        for copy in head_copies:
            copy.start()

    @pl.when(c == 0)
    def _():
        for copy in row_copies:
            copy.start()

    @pl.when(r == 0)
    def _():
        for copy in col_copies:
            copy.start()

    def loaded():
        @pl.when(c == 0)
        def _():
            for copy in row_copies:
                copy.wait()

        @pl.when(r == 0)
        def _():
            for copy in col_copies:
                copy.wait()

    neighbours = (along_x(1), along_y(1), along_x(3), along_y(3))

    def tree_copy(tree, chunk, way):
        rows = pl.ds(pl.multiple_of(LANES * tree + TREE_ROWS * (chunk % (TREE_CHUNKS // 2)), TREE_ROWS), TREE_ROWS)
        part = rowp.at[chunk // (TREE_CHUNKS // 2), :, rows, :]
        return pltpu.make_async_remote_copy(
            src_ref=part, dst_ref=part, send_sem=tree_send.at[way, chunk], recv_sem=tree_recv.at[tree, chunk],
            device_id=neighbours[way], device_id_type=MESH)

    chain_peers = (along_z(1), along_z(7), partner)

    def chain_copy(chunk, way):
        rows = pl.ds(pl.multiple_of(CHAIN_ROWS * (chunk % (CHAIN_CHUNKS // 2)), CHAIN_ROWS), CHAIN_ROWS)
        part = colp.at[chunk // (CHAIN_CHUNKS // 2), :, rows, :]
        return pltpu.make_async_remote_copy(
            src_ref=part, dst_ref=part, send_sem=chain_send.at[way, chunk], recv_sem=chain_recv.at[chunk],
            device_id=chain_peers[way], device_id_type=MESH)

    def small_copy(which, index, peer):
        return pltpu.make_async_remote_copy(
            src_ref=small.at[which], dst_ref=small.at[which], send_sem=small_send.at[which, index],
            recv_sem=small_recv.at[which], device_id=peer, device_id_type=MESH)

    def small_groups(which):
        z_steps = [small_copy(which, i, along_z(s)) for i, s in enumerate((3, 6, 2, 7, 1))]
        x_steps = [small_copy(which, 5 + i, along_x(s)) for i, s in enumerate((2, 1, 3))]
        y_steps = [small_copy(which, 8 + i, along_y(s)) for i, s in enumerate((2, 1, 3))]
        return (
            (root, z_steps), (edge & (z == 3), [z_steps[4]]), (edge & (z == 6), [z_steps[3]]),
            (edge, x_steps), ((y == 0) & (core == 0), y_steps), (core == 0, [small_copy(which, 11, partner)]))

    def small_forward(which):
        for condition, copies in small_groups(which):
            @pl.when(condition)
            def _():
                for copy in copies:
                    copy.start()

    def small_event(which):
        small_copy(which, 11, partner).wait_recv()
        small_forward(which)

    send_tree = [lookup(c, [entry + 1 for entry in send_table[way]]) - 1 for way in range(4)]
    chain_ways = (chain_up, chain_down, root | (on_chain & jnp.logical_not((r == 1) & (c == 0))))

    @pl.when(root)
    def _():
        lane = lax.broadcasted_iota(jnp.int32, (PANEL, LANES), 1)
        row = lax.broadcasted_iota(jnp.int32, (PANEL, LANES), 0)
        inside = lane < PANEL
        for copy in head_copies:
            copy.wait()

        tile_lane = lax.broadcasted_iota(jnp.int32, (8, LANES), 1)
        tile_row = lax.broadcasted_iota(jnp.int32, (8, LANES), 0)
        count = PANEL // 8
        real = [head[0, pl.ds(8 * t, 8), :] for t in range(count)]
        imag = [head[1, pl.ds(8 * t, 8), :] for t in range(count)]

        def down(value, j):
            return jnp.broadcast_to(value[j:j + 1, :], (8, LANES))

        def across(value, j):
            return jnp.broadcast_to(value[:, j:j + 1], (8, LANES))

        for k in range(0, PANEL, 2):
            tile, j = k // 8, k % 8
            first, second = tile_lane == k, tile_lane == k + 1
            col_a = [(across(real[t], k), across(imag[t], k)) for t in range(tile, count)]
            col_b = [(across(real[t], k + 1), across(imag[t], k + 1)) for t in range(tile, count)]
            pivot_a = down(col_a[0][0], j)
            off_real, off_imag = down(col_a[0][0], j + 1), down(col_a[0][1], j + 1)
            inv_a = 1.0 / pivot_a
            low_real, low_imag = off_real * inv_a, off_imag * inv_a
            pivot_b = down(col_b[0][0], j + 1) - (off_real * low_real + off_imag * low_imag)
            inv_b = 1.0 / pivot_b
            both = first | second
            a_real = jnp.where(both, jnp.where(first, 1.0, 0.0), down(real[tile], j))
            a_imag = jnp.where(both, 0.0, down(imag[tile], j))
            b_real = jnp.where(both, jnp.where(second, 1.0, 0.0), down(real[tile], j + 1))
            b_imag = jnp.where(both, 0.0, down(imag[tile], j + 1))
            b_real, b_imag = (
                b_real - (low_real * a_real - low_imag * a_imag), b_imag - (low_real * a_imag + low_imag * a_real))
            wb_real, wb_imag = b_real * inv_b, b_imag * inv_b
            wa_real = a_real * inv_a - (low_real * wb_real + low_imag * wb_imag)
            wa_imag = a_imag * inv_a - (low_real * wb_imag - low_imag * wb_real)
            for t in range(tile, count):
                (ar, ai), (br, bi) = col_a[t - tile], col_b[t - tile]
                next_real = jnp.where(both, 0.0, real[t]) - ((ar * wa_real - ai * wa_imag) + (br * wb_real - bi * wb_imag))
                next_imag = jnp.where(both, 0.0, imag[t]) - ((ar * wa_imag + ai * wa_real) + (br * wb_imag + bi * wb_real))
                if t == tile:
                    keep = tile_row < j
                    next_real = jnp.where(keep, real[t], jnp.where(tile_row == j, a_real, jnp.where(tile_row == j + 1, b_real, next_real)))
                    next_imag = jnp.where(keep, imag[t], jnp.where(tile_row == j, a_imag, jnp.where(tile_row == j + 1, b_imag, next_imag)))
                real[t], imag[t] = next_real, next_imag
            dv[pl.ds(k, 1), :] = pivot_a[0:1, :]
            dv[pl.ds(k + 1, 1), :] = pivot_b[0:1, :]

            if k == GREET_AT:
                loaded()
                answer()
                for chunk in range(TREE_CHUNKS):
                    for way in range(4):
                        tree_copy(way, chunk, way).start()
                for chunk in range(CHAIN_CHUNKS):
                    chain_copy(chunk, 2).start()

            if k == HEAD_AT:
                head_real = rowp[1, 0, pl.ds(0, PANEL), :]
                head_imag = rowp[1, 1, pl.ds(0, PANEL), :]
                small[0] = jnp.where(inside, jnp.where(lane <= row, head_real, head_imag), 0.0)
                pl.semaphore_wait(small_ready, 5)
                small_forward(0)

        pivots = dv[...]
        scale = lax.rsqrt(pivots)
        scale = scale * (1.5 - 0.5 * pivots * scale * scale)
        for t in range(count):
            lower = tile_lane <= tile_row + 8 * t
            rows = pl.ds(8 * t, 8)
            wr[rows, :] = jnp.where(lower, real[t], 0.0)
            wi[rows, :] = jnp.where(lower, imag[t], 0.0)
        wi[pl.ds(0, PANEL), :] = wi[pl.ds(0, PANEL), :] * scale
        wi[pl.ds(PANEL, LANES - PANEL), :] = jnp.zeros((LANES - PANEL, LANES), jnp.float32)
        small[1] = wr[...] * scale + wi[...].T[0:PANEL, :]
        small_forward(1)

    @pl.when(jnp.logical_not(root))
    def _():
        loaded()
        answer()
        depth = [lookup(c, depth_table[tree]) for tree in range(4)]
        way_start = [
            jnp.where((c == 0) | (send_tree[way] < 0), SLOTS, TREE_LAG * lookup(c, [
                depth_table[tree][chip] if tree >= 0 else 0 for chip, tree in enumerate(send_table[way])]))
            for way in range(4)]
        chain_depth = jnp.where(z <= 4, z, 8 - z)
        chain_now = (chain_up, on_chain & (z > 5), chain_ways[2])
        chain_depth_slots = CHAIN_LAG * chain_depth + CHAIN_START + jnp.where(z > 4, DOWN_START, 0)
        stage = jnp.where(z == 0, 0, jnp.where((z == 4) | (z == 5), 2, 1)) + jnp.where(x == 0, 0, 1) + jnp.where(y == 0, 0, 1)
        small_slot = SMALL_SLOT + STAGE_SLOTS * stage

        @pl.when(c == 0)
        def _():
            def source(chunk, carry):
                for way in range(4):
                    tree_copy(way, chunk, way).start()
                return carry

            lax.fori_loop(0, TREE_CHUNKS, source, 0)

        def slot(s, carry):
            for tree in range(4):
                chunk = s - TREE_LAG * depth[tree]

                @pl.when((c != 0) & (chunk >= 0) & (chunk < TREE_CHUNKS))
                def _():
                    tree_copy(tree, chunk, 0).wait_recv()

            for way in range(4):
                onward = s - way_start[way]

                @pl.when((onward >= 0) & (onward < TREE_CHUNKS))
                def _():
                    tree_copy(send_tree[way], onward, way).start()

            link = s - chain_depth_slots

            @pl.when(on_chain & (link >= 0) & (link < CHAIN_CHUNKS))
            def _():
                @pl.when((z != 0) | (c == 0))
                def _():
                    chain_copy(link, 0).wait_recv()

                @pl.when((link == 0) & chain_up)
                def _():
                    pl.semaphore_wait(chain_ready, 1)

                @pl.when((link == 0) & (z > 5))
                def _():
                    pl.semaphore_wait(chain_ready_down, 1)

                for way in range(3):
                    @pl.when(chain_now[way])
                    def _():
                        chain_copy(link, way).start()

            link_down = s - CHAIN_START - DOWN_START

            @pl.when(on_chain & (z == 0) & (link_down >= 0) & (link_down < CHAIN_CHUNKS))
            def _():
                @pl.when(link_down == 0)
                def _():
                    pl.semaphore_wait(chain_ready_down, 1)

                chain_copy(link_down, 1).start()

            @pl.when(s == small_slot)
            def _():
                @pl.when(edge & ((z == 3) | (z == 6)))
                def _():
                    pl.semaphore_wait(small_ready, 1)

                small_event(0)
                small_event(1)

            return carry

        lax.fori_loop(0, SLOTS, slot, 0)

        @pl.when(jnp.logical_not(on_chain))
        def _():
            def arrived(chunk, carry):
                chain_copy(chunk, 2).wait_recv()
                return carry

            lax.fori_loop(0, CHAIN_CHUNKS, arrived, 0)

    for way in range(4):
        @pl.when(send_tree[way] >= 0)
        def _():
            def sent(chunk, carry):
                tree_copy(0, chunk, way).wait_send()
                return carry

            lax.fori_loop(0, TREE_CHUNKS, sent, 0)

    for way in range(3):
        @pl.when(chain_ways[way])
        def _():
            def sent(chunk, carry):
                chain_copy(chunk, way).wait_send()
                return carry

            lax.fori_loop(0, CHAIN_CHUNKS, sent, 0)

    for which in range(2):
        for condition, copies in small_groups(which):
            @pl.when(condition)
            def _():
                for copy in copies:
                    copy.wait_send()


def halves(value):
    high = value.astype(jnp.bfloat16)
    return high, (value - high.astype(jnp.float32)).astype(jnp.bfloat16)


def product(left, right):
    (left_high, left_low), (right_high, right_low) = left, right

    def dot(a, b):
        return jnp.dot(a, b, preferred_element_type=jnp.float32)

    return dot(left_high, right_high) + (dot(left_low, right_high) + dot(left_high, right_low))


def block_matrix(a, b, c, d):
    return jnp.concatenate([jnp.concatenate([a, b], axis=1), jnp.concatenate([c, d], axis=1)], axis=0)


TILE = 256


def update(
    corr, fock, rowp_in, colp_in, small_in, over, transformed, panel, rowp, colp, small, cbuf, fbuf, pbuf,
    over_left, over_right, fock_left, fock_right, in_sem, out_sem, panel_sem,
):
    r, c = lax.axis_index("row"), lax.axis_index("col")
    pairs = (
        (small_in, small), (rowp_in.at[0], rowp.at[0]), (colp_in.at[0], colp.at[0]), (corr, cbuf),
        (rowp_in.at[1], rowp.at[1]), (colp_in.at[1], colp.at[1]), (fock, fbuf))
    loads = [pltpu.make_async_copy(src, dst, in_sem.at[i]) for i, (src, dst) in enumerate(pairs)]
    for load in loads:
        load.start()
    loads[0].wait()

    size = rowp.shape[2]
    width = colp.shape[3]
    row = lax.broadcasted_iota(jnp.int32, (LANES, LANES), 0)
    col = lax.broadcasted_iota(jnp.int32, (LANES, LANES), 1)
    rest = jnp.zeros((LANES - PANEL, LANES), jnp.float32)
    packed = jnp.concatenate([small[1], rest], axis=0)
    turned = packed.T
    inv_real = jnp.where(row >= col, packed, 0.0)
    inv_imag = jnp.where(row > col, turned, 0.0)
    inv_real_t = jnp.where(row <= col, turned, 0.0)
    inv_imag_t = jnp.where(row < col, packed, 0.0)
    right_adjoint = halves(block_matrix(inv_real_t, -inv_imag_t, inv_imag_t, inv_real_t))
    right_inverse = halves(block_matrix(inv_real, inv_imag, -inv_imag, inv_real))
    left_inverse = halves(block_matrix(inv_real, -inv_imag, inv_imag, inv_real))
    left_adjoint = halves(block_matrix(inv_real_t, inv_imag_t, -inv_imag_t, inv_real_t))

    gap = jnp.zeros((LANES - PANEL, width), jnp.float32)

    def top(which):
        return jnp.concatenate([colp[which, 0], gap, colp[which, 1], gap], axis=0)

    loads[1].wait()
    factor = product(halves(jnp.concatenate([rowp[0, 0], rowp[0, 1]], axis=1)), right_adjoint)
    pbuf[0] = factor[:, 0:LANES].T[0:PANEL]
    pbuf[1] = factor[:, LANES:2 * LANES].T[0:PANEL]
    panel_out = pltpu.make_async_copy(pbuf, panel, panel_sem)
    panel_out.start()
    over_left[0], over_left[1] = halves(factor)
    loads[2].wait()
    across = product(left_inverse, halves(top(0)))

    def right_side(value):
        real, imag = value[0:LANES], value[LANES:2 * LANES]
        return block_matrix(real, imag, -imag, real)

    over_right[0], over_right[1] = halves(right_side(across))

    out_copies = []

    def outer_tiles(left, right, buffer, target, which, sign):
        for tile in range(2 * width // TILE):
            part, cols = tile // (width // TILE), pl.ds(tile % (width // TILE) * TILE, TILE)
            columns = pl.ds(tile * TILE, TILE)
            piece = product((left[0], left[1]), (right[0, :, columns], right[1, :, columns]))
            old = buffer[part, :, cols]
            buffer[part, :, cols] = old + piece if sign > 0 else old - piece
            copy = pltpu.make_async_copy(buffer.at[part, :, cols], target.at[part, :, cols], out_sem.at[which, tile])
            copy.start()
            out_copies.append(copy)

    loads[3].wait()
    outer_tiles(over_left, over_right, cbuf, over, 0, -1)

    wide_row = lax.broadcasted_iota(jnp.int32, (size, 2 * LANES), 0) + r * size
    wide_lane = lax.broadcasted_iota(jnp.int32, (size, 2 * LANES), 1)
    unit = jnp.where((wide_row == wide_lane) & (wide_lane < PANEL), 1.0, 0.0)
    trans = product(halves(unit - factor), right_inverse)
    loads[4].wait()
    loads[5].wait()
    fock_left[0, :, 0:2 * LANES], fock_left[1, :, 0:2 * LANES] = halves(trans)
    fock_left[0, :, 2 * LANES:4 * LANES], fock_left[1, :, 2 * LANES:4 * LANES] = halves(jnp.concatenate([rowp[1, 0], rowp[1, 1]], axis=1))
    tall_row = lax.broadcasted_iota(jnp.int32, (2 * LANES, width), 0)
    tall_lane = lax.broadcasted_iota(jnp.int32, (2 * LANES, width), 1) + c * width
    unit = jnp.where((tall_row == tall_lane) & (tall_row < PANEL), 1.0, 0.0)
    trans_across = product(left_adjoint, halves(unit - across))

    packed = jnp.concatenate([small[0], rest], axis=0)
    turned = packed.T
    head_real = jnp.where(row >= col, packed, turned)
    head_imag = jnp.where(row < col, packed, jnp.where(row > col, -turned, 0.0))
    head = halves(block_matrix(head_real, -head_imag, head_imag, head_real))
    middle = top(1) + product(head, halves(trans_across))
    fock_right[0, 0:2 * LANES, :], fock_right[1, 0:2 * LANES, :] = halves(right_side(middle))
    fock_right[0, 2 * LANES:4 * LANES, :], fock_right[1, 2 * LANES:4 * LANES, :] = halves(right_side(trans_across))

    loads[6].wait()
    outer_tiles(fock_left, fock_right, fbuf, transformed, 1, 1)
    panel_out.wait()
    for copy in out_copies:
        copy.wait()


def shards(correlation, fock):
    rows, cols = correlation.shape[1:]
    f32, bf16 = jnp.float32, jnp.bfloat16
    hbm, vmem = pl.BlockSpec(memory_space=pl.ANY), pl.BlockSpec(memory_space=pltpu.VMEM)
    dma = pltpu.SemaphoreType.DMA
    rowp, colp, small = pl.pallas_call(
        spread,
        name="spread",
        out_shape=(
            jax.ShapeDtypeStruct((2, 2, rows, LANES), f32),
            jax.ShapeDtypeStruct((2, 2, PANEL, cols), f32),
            jax.ShapeDtypeStruct((2, PANEL, LANES), f32),
        ),
        in_specs=[hbm, hbm],
        out_specs=(vmem, vmem, vmem),
        scratch_shapes=[
            pltpu.VMEM((PANEL, LANES), f32),
            pltpu.VMEM((LANES, LANES), f32),
            pltpu.VMEM((PANEL, LANES), f32),
            pltpu.VMEM((2, PANEL, LANES), f32),
            dma((5,)),
            dma((4, TREE_CHUNKS)),
            dma((4, TREE_CHUNKS)),
            dma((3, CHAIN_CHUNKS)),
            dma((CHAIN_CHUNKS,)),
            dma((2, 12)),
            dma((2,)),
            pltpu.SemaphoreType.REGULAR,
            pltpu.SemaphoreType.REGULAR,
            pltpu.SemaphoreType.REGULAR,
        ],
        compiler_params=pltpu.CompilerParams(collective_id=0, has_side_effects=True),
    )(correlation, fock)
    reduced, transformed, panel = pl.pallas_call(
        update,
        name="update",
        out_shape=(
            jax.ShapeDtypeStruct((2, rows, cols), f32),
            jax.ShapeDtypeStruct((2, rows, cols), f32),
            jax.ShapeDtypeStruct((2, PANEL, rows), f32),
        ),
        in_specs=[hbm, hbm, hbm, hbm, hbm],
        out_specs=(hbm, hbm, hbm),
        scratch_shapes=[
            pltpu.VMEM((2, 2, rows, LANES), f32),
            pltpu.VMEM((2, 2, PANEL, cols), f32),
            pltpu.VMEM((2, PANEL, LANES), f32),
            pltpu.VMEM((2, rows, cols), f32),
            pltpu.VMEM((2, rows, cols), f32),
            pltpu.VMEM((2, PANEL, rows), f32),
            pltpu.VMEM((2, rows, 2 * LANES), bf16),
            pltpu.VMEM((2, 2 * LANES, 2 * cols), bf16),
            pltpu.VMEM((2, rows, 4 * LANES), bf16),
            pltpu.VMEM((2, 4 * LANES, 2 * cols), bf16),
            dma((7,)),
            dma((2, 2 * cols // TILE)),
            dma,
        ],
        compiler_params=pltpu.CompilerParams(vmem_limit_bytes=65 * 1000 * 1000),
    )(correlation, fock, rowp, colp, small)
    return reduced, transformed, jnp.swapaxes(panel, 1, 2)


def solution(mesh):
    in_specs = (P(None, "row", "col"), P(None, "row", "col"))
    out_specs = (P(None, "row", "col"), P(None, "row", "col"), P(None, "row", None))
    return jax.shard_map(shards, mesh=mesh, in_specs=in_specs, out_specs=out_specs, check_vma=False)
```

time: 50.4 us -> 39.5 us (0.78)
  the two profiles are of different devices: /device:TPU:139 before, /device:TPU:45 now
where the time goes in v2:
time: 39.5 us; the launch traced here: 39.2 us
  Pallas kernels  38.5 us (97%)
  between operations  0.64 us (2%)
    pallas_call x1, Pallas kernels, shards(): pl.pallas_call(spread, name='spread', out_shape=(jax.ShapeDtypeStruct((2,...  30.8 us
    pallas_call x1, Pallas kernels, shards(): pl.pallas_call(update, name='update', out_shape=(jax.ShapeDtypeStruct((2,...  7.75 us

profile of v2, /device:TPU:45, one launch (start us, length us, event | category | flops | bytes accessed | tf_op | source)
XLA Modules:
  0.0 39.2 jit_solution(13027601969367331114)
XLA Ops:
  0.6 30.8 %spread.1 = (f32[2,2,512,128]{3,2,1,0:T(8,128)}, f32[2,2,96,512]{3,2,1,0:T(8,128)}, f32[2,96,128]{2,1,0:T(8,128)}) custom-call(f32[2,512,512]{2,1,0:T(8,128)} %corr.3, f32[2,512,512]{2,1,0:T(8,128)} %fock.3), custom_call_target="tpu_custom_call" | custom-call | tf_op jit(solution)/shard_map/spread/pallas_call | solution.py:508
  31.4 7.7 %update.1 = (f32[2,512,512]{2,1,0:T(8,128)}, f32[2,512,512]{2,1,0:T(8,128)}, f32[2,96,512]{2,1,0:T(8,128)}) custom-call(f32[2,512,512]{2,1,0:T(8,128)} %corr.3, f32[2,512,512]{2,1,0:T(8,128)} %fock.3, f32[2,2,512,128]{3,2,1,0:T(8,128)} %get-tuple-element.9.rowp_in, f32[2,2,96,512]{3,2,1,0:T(8,128)} %get-tuple-element.10.colp_in, ...), custom_call_target="tpu_custom_call" | custom-call | tf_op jit(solution)/shard_map/update/pallas_call | solution.py:536

commit v3 on v2

--- a/solution.py
+++ b/solution.py
@@ -18,13 +18,14 @@
 CHAIN_ROWS = 16
 CHAIN_CHUNKS = 2 * PANEL // CHAIN_ROWS
 TREE_LAG = 5
-CHAIN_LAG = 5
-CHAIN_START = 3
+CHAIN_LAG = 4
+CHAIN_START = 0
 DOWN_START = 4
 STAGE_SLOTS = 5
 SMALL_SLOT = 9
-SLOTS = max(5 * TREE_LAG + TREE_CHUNKS, 4 * CHAIN_LAG + CHAIN_CHUNKS + CHAIN_START + DOWN_START, 4 * STAGE_SLOTS + SMALL_SLOT + 1)
-GREET_AT = 46
+EARLY_SLOTS = 5
+SLOTS = max(5 * TREE_LAG + TREE_CHUNKS, 4 * CHAIN_LAG + CHAIN_CHUNKS + CHAIN_START + DOWN_START, 4 * STAGE_SLOTS + SMALL_SLOT + EARLY_SLOTS + 1)
+GREET_AT = 30
 HEAD_AT = 78
 
 
@@ -57,7 +58,9 @@
     return value
 
 
-def spread(corr, fock, rowp, colp, small, wr, wi, dv, head, local_sem, tree_send, tree_recv, chain_send, chain_recv, small_send, small_recv, chain_ready, chain_ready_down, small_ready):
+def spread(
+    corr, fock, rowp_out, colp_out, small_out, rowp, colp, small, wr, wi, dv, head, local_sem, out_sem, tree_send, tree_recv, chain_send, chain_recv, small_send, small_recv, chain_ready, chain_ready_down, small_ready, small_ready_down,
+):
     r, c = lax.axis_index("row"), lax.axis_index("col")
     z, core = r // 2, r % 2
     y, x = c // 4, c % 4
@@ -84,31 +87,37 @@
     edge = (c == 0) & (core == 0)
     chain_up, chain_down = on_chain & (z < 4), on_chain & ((z == 0) | (z > 5))
     z_greetings = (
-        (chain_up, 1), (chain_down, 7),
-        (edge & ((z == 0) | (z == 3)), 1), (edge & (z == 0), 2), (edge & (z == 0), 3),
-        (edge & ((z == 0) | (z == 6)), 7), (edge & (z == 0), 6))
+        (on_chain & (z > 0) & (z < 4), 7), (on_chain & ((z == 5) | (z == 6)), 1),
+        (edge & (z == 1), 7), (edge & (z == 2), 6), (edge & (z == 3), 5),
+        (on_chain & (z == 3), 1), (on_chain & (z == 0), 7),
+        (edge & (z == 3), 1), (edge & (z == 0), 7), (edge & (z == 0), 6), (edge & (z == 6), 7))
     for condition, step in z_greetings:
         @pl.when(condition)
         def _():
             pl.semaphore_signal(barrier, inc=1, device_id=along_z(step), device_id_type=MESH)
 
-    heard = len(greeted) + jnp.where((z > 0) & (on_chain | edge), 1, 0)
+    heard = len(greeted) + jnp.where(on_chain & (z != 3) & (z != 5), 1, 0) + jnp.where(on_chain & (z == 7), 1, 0)
+    heard = heard + jnp.where(root, 3, 0) + jnp.where(edge & (z > 3), 1, 0)
 
     def answer():
         pl.semaphore_wait(barrier, heard)
 
-        @pl.when(on_chain & (z > 0) & (z <= 4))
+        @pl.when(on_chain & (z == 4))
         def _():
             pl.semaphore_signal(chain_ready, inc=1, device_id=along_z(7), device_id_type=MESH)
 
-        @pl.when(on_chain & (z > 4))
+        @pl.when(on_chain & (z == 7))
         def _():
             pl.semaphore_signal(chain_ready_down, inc=1, device_id=along_z(1), device_id_type=MESH)
 
-        @pl.when(edge & (z > 0))
-        def _():
-            back = jnp.where((z == 1) | (z == 4), 7, jnp.where(z == 2, 6, jnp.where(z == 3, 5, jnp.where(z == 6, 2, 1))))
-            pl.semaphore_signal(small_ready, inc=1, device_id=along_z(back), device_id_type=MESH)
+        @pl.when(edge & (z == 4))
+        def _():
+            pl.semaphore_signal(small_ready, inc=1, device_id=along_z(7), device_id_type=MESH)
+
+        @pl.when(edge & (z > 4))
+        def _():
+            back = jnp.where(z == 6, 2, 1)
+            pl.semaphore_signal(small_ready_down, inc=1, device_id=along_z(back), device_id_type=MESH)
 
     head_copies = [pltpu.make_async_copy(corr.at[:, pl.ds(0, PANEL), pl.ds(0, LANES)], head, local_sem.at[4])]
     row_copies = [pltpu.make_async_copy(src.at[:, :, pl.ds(0, LANES)], rowp.at[i], local_sem.at[i]) for i, src in enumerate((corr, fock))]
@@ -168,11 +177,12 @@
         x_steps = [small_copy(which, 5 + i, along_x(s)) for i, s in enumerate((2, 1, 3))]
         y_steps = [small_copy(which, 8 + i, along_y(s)) for i, s in enumerate((2, 1, 3))]
         return (
-            (root, z_steps), (edge & (z == 3), [z_steps[4]]), (edge & (z == 6), [z_steps[3]]),
-            (edge, x_steps), ((y == 0) & (core == 0), y_steps), (core == 0, [small_copy(which, 11, partner)]))
+            (root, [z_steps[0], z_steps[2], z_steps[4]]), (edge & (z == 3), [z_steps[4]]), (edge & (z == 6), [z_steps[3]]),
+            (edge, x_steps), ((y == 0) & (core == 0), y_steps), (core == 0, [small_copy(which, 11, partner)]),
+            (root, [z_steps[1], z_steps[3]]))
 
     def small_forward(which):
-        for condition, copies in small_groups(which):
+        for condition, copies in small_groups(which)[:-1]:
             @pl.when(condition)
             def _():
                 for copy in copies:
@@ -251,7 +261,6 @@
                 head_real = rowp[1, 0, pl.ds(0, PANEL), :]
                 head_imag = rowp[1, 1, pl.ds(0, PANEL), :]
                 small[0] = jnp.where(inside, jnp.where(lane <= row, head_real, head_imag), 0.0)
-                pl.semaphore_wait(small_ready, 5)
                 small_forward(0)
 
         pivots = dv[...]
@@ -266,6 +275,10 @@
         wi[pl.ds(PANEL, LANES - PANEL), :] = jnp.zeros((LANES - PANEL, LANES), jnp.float32)
         small[1] = wr[...] * scale + wi[...].T[0:PANEL, :]
         small_forward(1)
+        pl.semaphore_wait(small_ready_down, 2)
+        for which in (1, 0):
+            for copy in small_groups(which)[-1][1]:
+                copy.start()
 
     @pl.when(jnp.logical_not(root))
     def _():
@@ -280,7 +293,7 @@
         chain_now = (chain_up, on_chain & (z > 5), chain_ways[2])
         chain_depth_slots = CHAIN_LAG * chain_depth + CHAIN_START + jnp.where(z > 4, DOWN_START, 0)
         stage = jnp.where(z == 0, 0, jnp.where((z == 4) | (z == 5), 2, 1)) + jnp.where(x == 0, 0, 1) + jnp.where(y == 0, 0, 1)
-        small_slot = SMALL_SLOT + STAGE_SLOTS * stage
+        small_slot = SMALL_SLOT + STAGE_SLOTS * stage + jnp.where(z < 4, EARLY_SLOTS, 0)
 
         @pl.when(c == 0)
         def _():
@@ -314,13 +327,9 @@
                 def _():
                     chain_copy(link, 0).wait_recv()
 
-                @pl.when((link == 0) & chain_up)
+                @pl.when((link == 0) & (z == 3))
                 def _():
                     pl.semaphore_wait(chain_ready, 1)
-
-                @pl.when((link == 0) & (z > 5))
-                def _():
-                    pl.semaphore_wait(chain_ready_down, 1)
 
                 for way in range(3):
                     @pl.when(chain_now[way])
@@ -339,9 +348,13 @@
 
             @pl.when(s == small_slot)
             def _():
-                @pl.when(edge & ((z == 3) | (z == 6)))
+                @pl.when(edge & (z == 3))
                 def _():
                     pl.semaphore_wait(small_ready, 1)
+
+                @pl.when(edge & (z == 6))
+                def _():
+                    pl.semaphore_wait(small_ready_down, 1)
 
                 small_event(0)
                 small_event(1)
@@ -357,6 +370,12 @@
                 return carry
 
             lax.fori_loop(0, CHAIN_CHUNKS, arrived, 0)
+
+    flushes = [
+        pltpu.make_async_copy(src, dst, out_sem.at[i])
+        for i, (src, dst) in enumerate(((small, small_out), (rowp, rowp_out), (colp, colp_out)))]
+    for flush in flushes:
+        flush.start()
 
     for way in range(4):
         @pl.when(send_tree[way] >= 0)
@@ -382,6 +401,9 @@
             def _():
                 for copy in copies:
                     copy.wait_send()
+
+    for flush in flushes:
+        flush.wait()
 
 
 def halves(value):
@@ -477,8 +499,10 @@
     trans = product(halves(unit - factor), right_inverse)
     loads[4].wait()
     loads[5].wait()
-    fock_left[0, :, 0:2 * LANES], fock_left[1, :, 0:2 * LANES] = halves(trans)
-    fock_left[0, :, 2 * LANES:4 * LANES], fock_left[1, :, 2 * LANES:4 * LANES] = halves(jnp.concatenate([rowp[1, 0], rowp[1, 1]], axis=1))
+    left_real = jnp.concatenate([trans[:, 0:LANES], rowp[1, 0]], axis=1)
+    left_imag = jnp.concatenate([trans[:, LANES:2 * LANES], rowp[1, 1]], axis=1)
+    for i, value in enumerate((left_real, left_imag, left_real + left_imag)):
+        fock_left[0, i], fock_left[1, i] = halves(value)
     tall_row = lax.broadcasted_iota(jnp.int32, (2 * LANES, width), 0)
     tall_lane = lax.broadcasted_iota(jnp.int32, (2 * LANES, width), 1) + c * width
     unit = jnp.where((tall_row == tall_lane) & (tall_row < PANEL), 1.0, 0.0)
@@ -490,11 +514,23 @@
     head_imag = jnp.where(row < col, packed, jnp.where(row > col, -turned, 0.0))
     head = halves(block_matrix(head_real, -head_imag, head_imag, head_real))
     middle = top(1) + product(head, halves(trans_across))
-    fock_right[0, 0:2 * LANES, :], fock_right[1, 0:2 * LANES, :] = halves(right_side(middle))
-    fock_right[0, 2 * LANES:4 * LANES, :], fock_right[1, 2 * LANES:4 * LANES, :] = halves(right_side(trans_across))
+    right_real = jnp.concatenate([middle[0:LANES], trans_across[0:LANES]], axis=0)
+    right_imag = jnp.concatenate([middle[LANES:2 * LANES], trans_across[LANES:2 * LANES]], axis=0)
+    for i, value in enumerate((right_real, right_imag, right_real + right_imag)):
+        fock_right[0, i], fock_right[1, i] = halves(value)
 
     loads[6].wait()
-    outer_tiles(fock_left, fock_right, fbuf, transformed, 1, 1)
+    for tile in range(width // TILE):
+        cols = pl.ds(tile * TILE, TILE)
+        first, second, third = (
+            product((fock_left[0, i], fock_left[1, i]), (fock_right[0, i, :, cols], fock_right[1, i, :, cols])) for i in range(3))
+        fbuf[0, :, cols] = fbuf[0, :, cols] + (first - second)
+        fbuf[1, :, cols] = fbuf[1, :, cols] + ((third - first) - second)
+        for part in range(2):
+            copy = pltpu.make_async_copy(fbuf.at[part, :, cols], transformed.at[part, :, cols], out_sem.at[1, 2 * tile + part])
+            copy.start()
+            out_copies.append(copy)
+
     panel_out.wait()
     for copy in out_copies:
         copy.wait()
@@ -514,19 +550,24 @@
             jax.ShapeDtypeStruct((2, PANEL, LANES), f32),
         ),
         in_specs=[hbm, hbm],
-        out_specs=(vmem, vmem, vmem),
+        out_specs=(hbm, hbm, hbm),
         scratch_shapes=[
+            pltpu.VMEM((2, 2, rows, LANES), f32),
+            pltpu.VMEM((2, 2, PANEL, cols), f32),
+            pltpu.VMEM((2, PANEL, LANES), f32),
             pltpu.VMEM((PANEL, LANES), f32),
             pltpu.VMEM((LANES, LANES), f32),
             pltpu.VMEM((PANEL, LANES), f32),
             pltpu.VMEM((2, PANEL, LANES), f32),
             dma((5,)),
+            dma((3,)),
             dma((4, TREE_CHUNKS)),
             dma((4, TREE_CHUNKS)),
             dma((3, CHAIN_CHUNKS)),
             dma((CHAIN_CHUNKS,)),
             dma((2, 12)),
             dma((2,)),
+            pltpu.SemaphoreType.REGULAR,
             pltpu.SemaphoreType.REGULAR,
             pltpu.SemaphoreType.REGULAR,
             pltpu.SemaphoreType.REGULAR,
@@ -552,8 +593,8 @@
             pltpu.VMEM((2, PANEL, rows), f32),
             pltpu.VMEM((2, rows, 2 * LANES), bf16),
             pltpu.VMEM((2, 2 * LANES, 2 * cols), bf16),
-            pltpu.VMEM((2, rows, 4 * LANES), bf16),
-            pltpu.VMEM((2, 4 * LANES, 2 * cols), bf16),
+            pltpu.VMEM((2, 3, rows, 2 * LANES), bf16),
+            pltpu.VMEM((2, 3, 2 * LANES, cols), bf16),
             dma((7,)),
             dma((2, 2 * cols // TILE)),
             dma,

time: 39.5 us -> 37.7 us (0.954)
  Pallas kernels: 38.5 us -> 36.9 us
    pallas_call x1, Pallas kernels: 30.8 us -> 29.6 us  [shards(): pl.pallas_call(spread, name='spread', out_shape=(jax.ShapeDtypeStruct((2,...]
    pallas_call x1, Pallas kernels: 7.75 us -> 7.31 us  [shards(): pl.pallas_call(update, name='update', out_shape=(jax.ShapeDtypeStruct((2,...]
where the time goes in v3:
time: 37.7 us; the launch traced here: 37.6 us
  Pallas kernels  36.9 us (98%)
  between operations  0.64 us (2%)
    pallas_call x1, Pallas kernels, shards(): pl.pallas_call(spread, name='spread', out_shape=(jax.ShapeDtypeStruct((2,...  29.6 us
    pallas_call x1, Pallas kernels, shards(): pl.pallas_call(update, name='update', out_shape=(jax.ShapeDtypeStruct((2,...  7.31 us

profile of v3, /device:TPU:45, one launch (start us, length us, event | category | flops | bytes accessed | tf_op | source)
XLA Modules:
  0.0 37.6 jit_solution(13180369299087628786)
XLA Ops:
  0.6 29.6 %spread.1 = (f32[2,2,512,128]{3,2,1,0:T(8,128)}, f32[2,2,96,512]{3,2,1,0:T(8,128)}, f32[2,96,128]{2,1,0:T(8,128)}) custom-call(f32[2,512,512]{2,1,0:T(8,128)} %corr.3, f32[2,512,512]{2,1,0:T(8,128)} %fock.3), custom_call_target="tpu_custom_call" | custom-call | tf_op jit(solution)/shard_map/spread/pallas_call | solution.py:544
  30.2 7.3 %update.1 = (f32[2,512,512]{2,1,0:T(8,128)}, f32[2,512,512]{2,1,0:T(8,128)}, f32[2,96,512]{2,1,0:T(8,128)}) custom-call(f32[2,512,512]{2,1,0:T(8,128)} %corr.3, f32[2,512,512]{2,1,0:T(8,128)} %fock.3, f32[2,2,512,128]{3,2,1,0:T(8,128)} %get-tuple-element.9.rowp_in, f32[2,2,96,512]{3,2,1,0:T(8,128)} %get-tuple-element.10.colp_in, ...), custom_call_target="tpu_custom_call" | custom-call | tf_op jit(solution)/shard_map/update/pallas_call | solution.py:577

commit v4 on v3

--- a/solution.py
+++ b/solution.py
@@ -26,7 +26,10 @@
 EARLY_SLOTS = 5
 SLOTS = max(5 * TREE_LAG + TREE_CHUNKS, 4 * CHAIN_LAG + CHAIN_CHUNKS + CHAIN_START + DOWN_START, 4 * STAGE_SLOTS + SMALL_SLOT + EARLY_SLOTS + 1)
 GREET_AT = 30
-HEAD_AT = 78
+HEAD_AT = 32
+HEAD_DOWN_AT = 88
+HEAD_LEAD = 4
+HEAD_LEAD_DOWN = 1
 
 
 def rotated(x, y, turns):
@@ -263,6 +266,11 @@
                 small[0] = jnp.where(inside, jnp.where(lane <= row, head_real, head_imag), 0.0)
                 small_forward(0)
 
+            if k == HEAD_DOWN_AT:
+                pl.semaphore_wait(small_ready_down, 2)
+                for copy in small_groups(0)[-1][1]:
+                    copy.start()
+
         pivots = dv[...]
         scale = lax.rsqrt(pivots)
         scale = scale * (1.5 - 0.5 * pivots * scale * scale)
@@ -275,10 +283,8 @@
         wi[pl.ds(PANEL, LANES - PANEL), :] = jnp.zeros((LANES - PANEL, LANES), jnp.float32)
         small[1] = wr[...] * scale + wi[...].T[0:PANEL, :]
         small_forward(1)
-        pl.semaphore_wait(small_ready_down, 2)
-        for which in (1, 0):
-            for copy in small_groups(which)[-1][1]:
-                copy.start()
+        for copy in small_groups(1)[-1][1]:
+            copy.start()
 
     @pl.when(jnp.logical_not(root))
     def _():
@@ -293,7 +299,9 @@
         chain_now = (chain_up, on_chain & (z > 5), chain_ways[2])
         chain_depth_slots = CHAIN_LAG * chain_depth + CHAIN_START + jnp.where(z > 4, DOWN_START, 0)
         stage = jnp.where(z == 0, 0, jnp.where((z == 4) | (z == 5), 2, 1)) + jnp.where(x == 0, 0, 1) + jnp.where(y == 0, 0, 1)
-        small_slot = SMALL_SLOT + STAGE_SLOTS * stage + jnp.where(z < 4, EARLY_SLOTS, 0)
+        middle = (z > 0) & (z < 5)
+        small_slot = SMALL_SLOT + STAGE_SLOTS * stage + jnp.where(z < 4, EARLY_SLOTS, 0) - jnp.where(middle, stage + 1, 0)
+        head_slot = small_slot - jnp.where(z < 5, HEAD_LEAD, HEAD_LEAD_DOWN)
 
         @pl.when(c == 0)
         def _():
@@ -346,7 +354,7 @@
 
                 chain_copy(link_down, 1).start()
 
-            @pl.when(s == small_slot)
+            @pl.when(s == head_slot)
             def _():
                 @pl.when(edge & (z == 3))
                 def _():
@@ -357,6 +365,9 @@
                     pl.semaphore_wait(small_ready_down, 1)
 
                 small_event(0)
+
+            @pl.when(s == small_slot)
+            def _():
                 small_event(1)
 
             return carry

time: 37.7 us -> 37.3 us (0.989)
  Pallas kernels: 36.9 us -> 36.2 us
    pallas_call x1, Pallas kernels: 29.6 us -> 28.9 us  [shards(): pl.pallas_call(spread, name='spread', out_shape=(jax.ShapeDtypeStruct((2,...]
where the time goes in v4:
time: 37.3 us; the launch traced here: 36.9 us
  Pallas kernels  36.2 us (97%)
  between operations  0.64 us (2%)
    pallas_call x1, Pallas kernels, shards(): pl.pallas_call(spread, name='spread', out_shape=(jax.ShapeDtypeStruct((2,...  28.9 us
    pallas_call x1, Pallas kernels, shards(): pl.pallas_call(update, name='update', out_shape=(jax.ShapeDtypeStruct((2,...  7.32 us

profile of v4, /device:TPU:45, one launch (start us, length us, event | category | flops | bytes accessed | tf_op | source)
XLA Modules:
  0.0 36.9 jit_solution(7884301987282504443)
XLA Ops:
  0.6 28.9 %spread.1 = (f32[2,2,512,128]{3,2,1,0:T(8,128)}, f32[2,2,96,512]{3,2,1,0:T(8,128)}, f32[2,96,128]{2,1,0:T(8,128)}) custom-call(f32[2,512,512]{2,1,0:T(8,128)} %corr.3, f32[2,512,512]{2,1,0:T(8,128)} %fock.3), custom_call_target="tpu_custom_call" | custom-call | tf_op jit(solution)/shard_map/spread/pallas_call | solution.py:555
  29.6 7.3 %update.1 = (f32[2,512,512]{2,1,0:T(8,128)}, f32[2,512,512]{2,1,0:T(8,128)}, f32[2,96,512]{2,1,0:T(8,128)}) custom-call(f32[2,512,512]{2,1,0:T(8,128)} %corr.3, f32[2,512,512]{2,1,0:T(8,128)} %fock.3, f32[2,2,512,128]{3,2,1,0:T(8,128)} %get-tuple-element.9.rowp_in, f32[2,2,96,512]{3,2,1,0:T(8,128)} %get-tuple-element.10.colp_in, ...), custom_call_target="tpu_custom_call" | custom-call | tf_op jit(solution)/shard_map/update/pallas_call | solution.py:588

commit v5 on v4

--- a/solution.py
+++ b/solution.py
@@ -197,6 +197,9 @@
 
     send_tree = [lookup(c, [entry + 1 for entry in send_table[way]]) - 1 for way in range(4)]
     chain_ways = (chain_up, chain_down, root | (on_chain & jnp.logical_not((r == 1) & (c == 0))))
+
+    first_flush = pltpu.make_async_copy(rowp.at[0], rowp_out.at[0], out_sem.at[3])
+    flush_slot = 5 * TREE_LAG + TREE_CHUNKS // 2
 
     @pl.when(root)
     def _():
@@ -285,6 +288,7 @@
         small_forward(1)
         for copy in small_groups(1)[-1][1]:
             copy.start()
+        first_flush.start()
 
     @pl.when(jnp.logical_not(root))
     def _():
@@ -354,6 +358,10 @@
 
                 chain_copy(link_down, 1).start()
 
+            @pl.when(s == flush_slot)
+            def _():
+                first_flush.start()
+
             @pl.when(s == head_slot)
             def _():
                 @pl.when(edge & (z == 3))
@@ -384,7 +392,7 @@
 
     flushes = [
         pltpu.make_async_copy(src, dst, out_sem.at[i])
-        for i, (src, dst) in enumerate(((small, small_out), (rowp, rowp_out), (colp, colp_out)))]
+        for i, (src, dst) in enumerate(((small, small_out), (rowp.at[1], rowp_out.at[1]), (colp, colp_out)))]
     for flush in flushes:
         flush.start()
 
@@ -413,7 +421,7 @@
                 for copy in copies:
                     copy.wait_send()
 
-    for flush in flushes:
+    for flush in [first_flush] + flushes:
         flush.wait()
 
 
@@ -571,7 +579,7 @@
             pltpu.VMEM((PANEL, LANES), f32),
             pltpu.VMEM((2, PANEL, LANES), f32),
             dma((5,)),
-            dma((3,)),
+            dma((4,)),
             dma((4, TREE_CHUNKS)),
             dma((4, TREE_CHUNKS)),
             dma((3, CHAIN_CHUNKS)),

time: 37.3 us -> 37.1 us (level)
  no operation moved by 1% of the time
where the time goes in v5:
time: 37.1 us; the launch traced here: 36.7 us
  Pallas kernels  36.1 us (97%)
  between operations  0.64 us (2%)
    pallas_call x1, Pallas kernels, shards(): pl.pallas_call(spread, name='spread', out_shape=(jax.ShapeDtypeStruct((2,...  28.8 us
    pallas_call x1, Pallas kernels, shards(): pl.pallas_call(update, name='update', out_shape=(jax.ShapeDtypeStruct((2,...  7.32 us

profile of v5, /device:TPU:45, one launch (start us, length us, event | category | flops | bytes accessed | tf_op | source)
XLA Modules:
  0.0 36.7 jit_solution(2758776362174179122)
XLA Ops:
  0.6 28.8 %spread.1 = (f32[2,2,512,128]{3,2,1,0:T(8,128)}, f32[2,2,96,512]{3,2,1,0:T(8,128)}, f32[2,96,128]{2,1,0:T(8,128)}) custom-call(f32[2,512,512]{2,1,0:T(8,128)} %corr.3, f32[2,512,512]{2,1,0:T(8,128)} %fock.3), custom_call_target="tpu_custom_call" | custom-call | tf_op jit(solution)/shard_map/spread/pallas_call | solution.py:563
  29.4 7.3 %update.1 = (f32[2,512,512]{2,1,0:T(8,128)}, f32[2,512,512]{2,1,0:T(8,128)}, f32[2,96,512]{2,1,0:T(8,128)}) custom-call(f32[2,512,512]{2,1,0:T(8,128)} %corr.3, f32[2,512,512]{2,1,0:T(8,128)} %fock.3, f32[2,2,512,128]{3,2,1,0:T(8,128)} %get-tuple-element.9.rowp_in, f32[2,2,96,512]{3,2,1,0:T(8,128)} %get-tuple-element.10.colp_in, ...), custom_call_target="tpu_custom_call" | custom-call | tf_op jit(solution)/shard_map/update/pallas_call | solution.py:596
